TPU v7x, 32 devices: a whole 2x2x4 slice. The times are simulated.
32 devices in a mesh: tm: 16 (over z, y, x), seq: 2 (over core).
Axes of the slice: x: 2, y: 2, z: 4, core: 2. Of those that a mesh axis runs over, the one named last changes fastest.
Arguments:
- gains: float32 [128, 128, 128], P(('seq', 'tm')), parts along dimension 0, may hold values from -1 to 1
- offsets: float32 [128, 128], P(('seq', 'tm')), parts along dimension 0, may hold values from -8 to 8
- cov_terms: float32 [128, 128, 128], P(('seq', 'tm')), parts along dimension 0, as said below
Outputs:
- smoothed_means: float32 [128, 128], P(('seq', 'tm')), parts along dimension 0
- smoothed_covs: float32 [128, 128, 128], P(('seq', 'tm')), parts along dimension 0
- moments: float32 [256, 128], P('seq'), parts along dimension 0
There are 2 independent parts, one for each index of `seq`. A program takes and returns all parts, laid end to end along the dimension named above; each array names one. Nothing has to cross between parts.
Inputs may be any that keep to these rules, and one draw needn't show every extreme that they name: `cov_terms`: each step's covariance term is symmetric positive definite.
All inputs are finite; a program needn't handle non-finite values.
Results may differ from a plain program's by a relative error of at most 0.00014.
Values sent between devices are 32-bit elements; how exact they have to be, the bound alone decides.
A program may use at most 128 MiB of HBM per device.

v0:
```python
import jax
import jax.numpy as jnp
from jax import lax
from jax.sharding import PartitionSpec as P


def prefix(part, axis, combine, identity):
    count = lax.axis_size(axis)
    place = lax.axis_index(axis)
    ahead = count - 1 - place
    gathered = jax.tree.map(lambda a: lax.all_gather(a, axis), part)
    state = jax.tree.map(lambda a, e: jnp.zeros_like(a) + jnp.asarray(e, a.dtype), part, identity)

    def one(lap, state):
        source = count - 1 - lap
        return combine(
            state, jax.tree.map(lambda a: lax.dynamic_index_in_dim(a, source, 0, False), gathered)
        )

    return lax.fori_loop(0, ahead, one, state)


def product(left, right):
    return jnp.dot(left, right, precision=lax.Precision.HIGHEST, preferred_element_type=jnp.float32)


def compose(earlier, following):
    gain_left, offset_left, prior_spread_matrix = earlier
    gain_right, offset_right, cov_right = following
    gain = product(gain_left, gain_right)
    offset = offset_left + product(gain_left, offset_right)
    covariance = prior_spread_matrix + product(product(gain_left, cov_right), gain_left.T)
    return (gain, offset, covariance)


def join_higher(higher, lower):
    return compose(lower, higher)


def drop_suffix(boundary, element):
    merged = compose(element, boundary)
    return (merged, None)


def walk(state_pair, element):
    upcoming_average, cov_next = state_pair
    gain, offset, covariance = element
    mean_now = offset + product(gain, upcoming_average)
    cov_now = covariance + product(product(gain, cov_next), gain.T)
    return ((mean_now, cov_now), (mean_now, cov_now))


def local(gains, offsets, cov_terms):
    devices = lax.axis_size("tm")
    position = lax.axis_index("tm")
    local_steps = gains.shape[0]
    width = gains.shape[1]
    final_step = jnp.logical_and(
        jnp.arange(local_steps) == local_steps - 1, position == devices - 1
    )
    gains = jnp.where(final_step[:, None, None], jnp.zeros_like(gains), gains)
    unit = (
        jnp.eye(width, dtype=jnp.float32),
        jnp.zeros((width,), jnp.float32),
        jnp.zeros((width, width), jnp.float32),
    )
    aggregate, unused = lax.scan(drop_suffix, unit, (gains, offsets, cov_terms), reverse=True)
    boundary = prefix((aggregate[0], aggregate[1], aggregate[2]), "tm", join_higher, unit)
    final_pair, outputs = lax.scan(
        walk, (boundary[1], boundary[2]), (gains, offsets, cov_terms), reverse=True
    )
    mean_rows, cov_rows = outputs
    local_moment = jnp.sum(cov_rows, axis=0) + product(mean_rows.T, mean_rows)
    total_moment = lax.psum(local_moment, "tm")
    moments = total_moment / (local_steps * devices)
    return (mean_rows, cov_rows, moments)


def solution(mesh):
    in_specs = (P(("seq", "tm"), None, None), P(("seq", "tm"), None), P(("seq", "tm"), None, None))
    out_specs = (P(("seq", "tm"), None), P(("seq", "tm"), None, None), P("seq", None))
    return jax.shard_map(local, mesh=mesh, in_specs=in_specs, out_specs=out_specs, check_vma=False)
```

profile of v0, /device:TPU:0, one launch (start us, length us, event | category | flops | bytes accessed | tf_op | source)
XLA Modules:
  0.0 288.2 jit_solution(3906093262499196804)
XLA Ops:
  7.3 1.1 broadcast_select_fusion.1
  8.4 3.9 %while.57 = (s32[]{:T(128)}, f32[128,128]{1,0:T(8,128)S(1)}, f32[128]{0:T(128)S(1)}, f32[128,128]{1,0:T(8,128)S(1)}, f32[4,128,128]{2,1,0:T(8,128)S(1)}, /*index...) while((s32[]{:T(128)}, f32[128,128]{1,0:T(8,128)S(1)}, ...), condition=%wide.region_1.2_spmd.clone, body=%wide.region_0.1_spmd.clone.sunk | while | flops 75727104 | bytes 857219 | solution.py:67
  8.6 0.3 convolution_add_fusion.7
  10.6 0.3 convolution_add_fusion.7
  12.3 0.6 copy-done
  13.0 0.7 all-gather.9.cloned.1.call-update
  13.7 42.2 %all-gather.3 = f32[16,1,128]{2,1,0:T(1,128)S(1)} all-gather(f32[1,1,128]{2,1,0:T(1,128)S(1)} %bitcast.141), channel_id=2, replica_groups=mesh['tm'=16,'seq'=2] {'tm'}, dimensions={0}, use_global_device_ids=true | all-gather | bytes 8704 | tf_op jit(solution)/shard_map/all_gather | solution.py:11
  55.9 15.2 %all-gather.7.cloned.1.call-done = f32[2048,128]{1,0:T(8,128)} async-done(((f32[128,128]{1,0:T(8,128)}), f32[2048,128]{1,0:T(8,128)}) %all-gather.7.cloned.1.call-update) | async-done | bytes 1048592 | tf_op jit(solution)/shard_map/all_gather | solution.py:11
  71.1 57.4 %all-gather.9.cloned.1.call-done = f32[2048,128]{1,0:T(8,128)} async-done(((f32[128,128]{1,0:T(8,128)}), f32[2048,128]{1,0:T(8,128)}) %all-gather.9.cloned.1.call-update) | async-done | bytes 1048592 | tf_op jit(solution)/shard_map/all_gather | solution.py:11
  128.5 49.0 %while.55 = (s32[]{:T(128)}, f32[128]{0:T(128)S(1)}, f32[128,128]{1,0:T(8,128)S(1)}, s32[]{:T(128)}, f32[16,128]{1,0:T(8,128)S(1)}, /*index=5*/f32[16,128,128]{2...) while((s32[]{:T(128)}, f32[128]{0:T(128)S(1)}, ...), condition=%wide.region_3.4_spmd, body=%wide.region_2.3_spmd.sunk | while | flops 50544772 | bytes 529055 | solution.py:20
  128.5 1.0 fusion.92
  129.6 1.1 convolution_add_fusion.6
  130.7 1.0 fusion.91
  131.7 1.1 fusion.92
  132.8 1.1 convolution_add_fusion.6
  134.0 1.0 fusion.91
  135.0 1.1 fusion.92
  136.1 1.1 convolution_add_fusion.6
  137.3 1.0 fusion.91
  138.3 1.1 fusion.92
  139.4 1.1 convolution_add_fusion.6
  140.5 1.0 fusion.91
  141.6 1.1 fusion.92
  142.7 1.1 convolution_add_fusion.6
  143.8 1.0 fusion.91
  144.8 1.1 fusion.92
  145.9 1.1 convolution_add_fusion.6
  147.1 1.0 fusion.91
  148.1 1.1 fusion.92
  149.2 1.1 convolution_add_fusion.6
  150.3 1.0 fusion.91
  151.4 1.1 fusion.92
  152.5 1.1 convolution_add_fusion.6
  153.6 1.0 fusion.91
  154.6 1.1 fusion.92
  155.7 1.1 convolution_add_fusion.6
  156.9 1.0 fusion.91
  157.9 1.1 fusion.92
  159.0 1.1 convolution_add_fusion.6
  160.2 1.0 fusion.91
  161.2 1.1 fusion.92
  162.3 1.1 convolution_add_fusion.6
  163.4 1.0 fusion.91
  164.5 1.1 fusion.92
  165.6 1.1 convolution_add_fusion.6
  166.7 1.0 fusion.91
  167.7 1.1 fusion.92
  168.8 1.1 convolution_add_fusion.6
  170.0 1.0 fusion.91
  171.0 1.1 fusion.92
  172.1 1.1 convolution_add_fusion.6
  173.2 1.0 fusion.91
  174.3 1.1 fusion.92
  175.4 1.1 convolution_add_fusion.6
  176.5 1.0 fusion.91
  177.6 3.0 %while.56 = (s32[]{:T(128)}, f32[128]{0:T(128)S(1)}, f32[128,128]{1,0:T(8,128)S(1)}, f32[4,128]{1,0:T(4,128)S(1)}, f32[4,128,128]{2,1,0:T(8,128)S(1)}, /*index=5...) while((s32[]{:T(128)}, f32[128]{0:T(128)S(1)}, ...), condition=%wide.region_5.6_spmd, body=%wide.region_4.5_spmd.sunk | while | flops 50544768 | bytes 595585 | solution.py:69
  177.8 0.3 bitcast_dynamic-update-slice_fusion.2
  178.6 0.3 bitcast_dynamic-update-slice_fusion.2
  179.4 0.3 bitcast_dynamic-update-slice_fusion.2
  180.1 0.3 bitcast_dynamic-update-slice_fusion.2
  180.7 0.5 copy-done.4
  181.2 0.9 convolution_add_fusion.3
  182.2 98.0 %all-reduce.2.cloned.1.call-done = f32[128,128]{1,0:T(8,128)} async-done(((f32[128,128]{1,0:T(8,128)}), f32[128,128]{1,0:T(8,128)}) %all-reduce.2.cloned.1.call-update) | async-done | bytes 65552 | tf_op jit(solution)/shard_map/psum | solution.py:74
  280.2 1.5 broadcast_multiply_fusion
  (77 shorter events, 5.2 us)
Async XLA Ops:
  7.2 63.9 %all-gather.7.cloned.1.call-start = ((), (), s32[]{:S(2)}) async-start(), calls=%async_computation.1 | async-start | bytes 1114112 | tf_op jit(solution)/shard_map/all_gather | solution.py:11
  7.3 1.1 copy-start.2
  7.3 1.1 copy-start.5
  12.3 0.6 copy-start
  12.3 0.7 copy-start.1
  12.9 115.6 %all-gather.9.cloned.1.call-start = ((), (), s32[]{:S(2)}) async-start(), calls=%async_computation.2 | async-start | bytes 1114112 | tf_op jit(solution)/shard_map/all_gather | solution.py:11
  13.7 266.5 %all-reduce.2.cloned.1.call-start = ((), (), s32[]{:S(2)}) async-start(), calls=%async_computation | async-start | bytes 131072 | tf_op jit(solution)/shard_map/psum | solution.py:74
  180.7 0.6 copy-start.4
  180.7 1.5 copy-start.3
Sparse Core Ops, SparseCore 0:
  13.0 57.9 all-gather.6
  74.4 54.0 all-gather.8
  182.3 97.8 all-reduce.1
where the time goes:
time: 291 us; the launch traced here: 288 us
  waiting for transfers between devices  171 us (59%)
  matrix products  55.8 us (19%)
  blocking collectives  42.2 us (15%)
  between operations  13.9 us (5%)
    psum x1, waiting for transfers between devices, local(): total_moment = lax.psum(local_moment, 'tm')  98 us
    all_gather x2, waiting for transfers between devices, prefix(): gathered = jax.tree.map(lambda a: lax.all_gather(a, axis), part)  72.6 us
    dot_general x74, matrix products, product(): jnp.dot(left, right, precision=lax.Precision.HIGHEST, preferred_element_t...  55.8 us
    all_gather x1, blocking collectives, prefix(): gathered = jax.tree.map(lambda a: lax.all_gather(a, axis), part)  42.2 us
  transfers between devices with their start and end apart: 3, of which 3 were waited for; matrix products, arithmetic and copies ran while one was open for 0% of the time, Pallas kernels for 0%

commit v1 on v0

--- a/solution.py
+++ b/solution.py
@@ -71,7 +71,8 @@
     )
     mean_rows, cov_rows = outputs
     local_moment = jnp.sum(cov_rows, axis=0) + product(mean_rows.T, mean_rows)
-    total_moment = lax.psum(local_moment, "tm")
+    current_arr = lax.all_gather(local_moment, "tm")
+    total_moment = jnp.sum(current_arr, axis=0)
     moments = total_moment / (local_steps * devices)
     return (mean_rows, cov_rows, moments)
 

time: 291 us -> 244 us (0.84)
  waiting for transfers between devices: 171 us -> 125 us
    psum x1 -> x0, waiting for transfers between devices: 98 us -> none  [local(): total_moment = lax.psum(local_moment, 'tm')]
    all_gather x0 -> x1, waiting for transfers between devices: none -> 51.3 us  [local(): current_arr = lax.all_gather(local_moment, 'tm')]
where the time goes in v1:
time: 244 us; the launch traced here: 242 us
  waiting for transfers between devices  125 us (51%)
  matrix products  55.8 us (23%)
  blocking collectives  42.2 us (17%)
  between operations  13.9 us (6%)
  other arithmetic  3.04 us (1%)
    all_gather x2, waiting for transfers between devices, prefix(): gathered = jax.tree.map(lambda a: lax.all_gather(a, axis), part)  72.6 us
    dot_general x74, matrix products, product(): jnp.dot(left, right, precision=lax.Precision.HIGHEST, preferred_element_t...  55.8 us
    all_gather x1, waiting for transfers between devices, local(): current_arr = lax.all_gather(local_moment, 'tm')  51.3 us
    all_gather x1, blocking collectives, prefix(): gathered = jax.tree.map(lambda a: lax.all_gather(a, axis), part)  42.2 us
  transfers between devices with their start and end apart: 3, of which 3 were waited for; matrix products, arithmetic and copies ran while one was open for 0% of the time, Pallas kernels for 0%

profile of v1, /device:TPU:0, one launch (start us, length us, event | category | flops | bytes accessed | tf_op | source)
XLA Modules:
  0.0 241.9 jit_solution(14477430081322075973)
XLA Ops:
  7.3 1.1 broadcast_select_fusion.1
  8.4 3.9 %while.57 = (s32[]{:T(128)}, f32[128,128]{1,0:T(8,128)S(1)}, f32[128]{0:T(128)S(1)}, f32[128,128]{1,0:T(8,128)S(1)}, f32[4,128,128]{2,1,0:T(8,128)S(1)}, /*index...) while((s32[]{:T(128)}, f32[128,128]{1,0:T(8,128)S(1)}, ...), condition=%wide.region_1.2_spmd.clone, body=%wide.region_0.1_spmd.clone.sunk | while | flops 75727104 | bytes 857219 | solution.py:67
  8.6 0.3 convolution_add_fusion.7
  12.3 0.6 copy-done
  13.0 0.7 all-gather.11.cloned.1.call-update
  13.7 42.2 %all-gather.4 = f32[16,1,128]{2,1,0:T(1,128)S(1)} all-gather(f32[1,1,128]{2,1,0:T(1,128)S(1)} %bitcast.143), channel_id=2, replica_groups=mesh['tm'=16,'seq'=2] {'tm'}, dimensions={0}, use_global_device_ids=true | all-gather | bytes 8704 | tf_op jit(solution)/shard_map/all_gather | solution.py:11
  55.9 15.2 %all-gather.9.cloned.1.call-done = f32[2048,128]{1,0:T(8,128)} async-done(((f32[128,128]{1,0:T(8,128)}), f32[2048,128]{1,0:T(8,128)}) %all-gather.9.cloned.1.call-update) | async-done | bytes 1048592 | tf_op jit(solution)/shard_map/all_gather | solution.py:11
  71.1 57.4 %all-gather.11.cloned.1.call-done = f32[2048,128]{1,0:T(8,128)} async-done(((f32[128,128]{1,0:T(8,128)}), f32[2048,128]{1,0:T(8,128)}) %all-gather.11.cloned.1.call-update) | async-done | bytes 1048592 | tf_op jit(solution)/shard_map/all_gather | solution.py:11
  128.5 49.0 %while.55 = (s32[]{:T(128)}, f32[128]{0:T(128)S(1)}, f32[128,128]{1,0:T(8,128)S(1)}, s32[]{:T(128)}, f32[16,128]{1,0:T(8,128)S(1)}, /*index=5*/f32[16,128,128]{2...) while((s32[]{:T(128)}, f32[128]{0:T(128)S(1)}, ...), condition=%wide.region_3.4_spmd, body=%wide.region_2.3_spmd.sunk | while | flops 50544772 | bytes 529055 | solution.py:20
  128.5 1.0 fusion.92
  129.6 1.1 convolution_add_fusion.6
  130.7 1.0 fusion.91
  131.7 1.1 fusion.92
  132.8 1.1 convolution_add_fusion.6
  134.0 1.0 fusion.91
  135.0 1.1 fusion.92
  136.1 1.1 convolution_add_fusion.6
  137.3 1.0 fusion.91
  138.3 1.1 fusion.92
  139.4 1.1 convolution_add_fusion.6
  140.5 1.0 fusion.91
  141.6 1.1 fusion.92
  142.6 1.1 convolution_add_fusion.6
  143.8 1.0 fusion.91
  144.8 1.1 fusion.92
  145.9 1.1 convolution_add_fusion.6
  147.1 1.0 fusion.91
  148.1 1.1 fusion.92
  149.2 1.1 convolution_add_fusion.6
  150.3 1.0 fusion.91
  151.4 1.1 fusion.92
  152.5 1.1 convolution_add_fusion.6
  153.6 1.0 fusion.91
  154.6 1.1 fusion.92
  155.7 1.1 convolution_add_fusion.6
  156.9 1.0 fusion.91
  157.9 1.1 fusion.92
  159.0 1.1 convolution_add_fusion.6
  160.2 1.0 fusion.91
  161.2 1.1 fusion.92
  162.3 1.1 convolution_add_fusion.6
  163.4 1.0 fusion.91
  164.5 1.1 fusion.92
  165.5 1.1 convolution_add_fusion.6
  166.7 1.0 fusion.91
  167.7 1.1 fusion.92
  168.8 1.1 convolution_add_fusion.6
  170.0 1.0 fusion.91
  171.0 1.1 fusion.92
  172.1 1.1 convolution_add_fusion.6
  173.2 1.1 fusion.91
  174.3 1.0 fusion.92
  175.4 1.1 convolution_add_fusion.6
  176.5 1.0 fusion.91
  177.6 3.0 %while.56 = (s32[]{:T(128)}, f32[128]{0:T(128)S(1)}, f32[128,128]{1,0:T(8,128)S(1)}, f32[4,128]{1,0:T(4,128)S(1)}, f32[4,128,128]{2,1,0:T(8,128)S(1)}, /*index=5...) while((s32[]{:T(128)}, f32[128]{0:T(128)S(1)}, ...), condition=%wide.region_5.6_spmd, body=%wide.region_4.5_spmd.sunk | while | flops 50544768 | bytes 595585 | solution.py:69
  177.8 0.3 bitcast_dynamic-update-slice_fusion.2
  178.6 0.3 bitcast_dynamic-update-slice_fusion.2
  179.4 0.3 bitcast_dynamic-update-slice_fusion.2
  180.1 0.3 bitcast_dynamic-update-slice_fusion.2
  180.7 0.5 copy-done.4
  181.2 0.9 convolution_add_fusion.3
  182.2 51.3 %all-gather.13.cloned.1.call-done = f32[2048,128]{1,0:T(8,128)} async-done(((f32[128,128]{1,0:T(8,128)}), f32[2048,128]{1,0:T(8,128)}) %all-gather.13.cloned.1.call-update) | async-done | bytes 1048592 | tf_op jit(solution)/shard_map/all_gather | solution.py:74
  233.5 1.3 reduce_sum.19
  234.8 0.6 broadcast_multiply_fusion
  (78 shorter events, 5.5 us)
Async XLA Ops:
  7.2 63.9 %all-gather.9.cloned.1.call-start = ((), (), s32[]{:S(2)}) async-start(), calls=%async_computation | async-start | bytes 1114112 | tf_op jit(solution)/shard_map/all_gather | solution.py:11
  7.3 1.1 copy-start.2
  7.3 1.1 copy-start.5
  12.3 0.6 copy-start
  12.3 0.7 copy-start.1
  12.9 115.6 %all-gather.11.cloned.1.call-start = ((), (), s32[]{:S(2)}) async-start(), calls=%async_computation.1 | async-start | bytes 1114112 | tf_op jit(solution)/shard_map/all_gather | solution.py:11
  13.7 219.8 %all-gather.13.cloned.1.call-start = ((), (), s32[]{:S(2)}) async-start(), calls=%async_computation.2 | async-start | bytes 1114112 | tf_op jit(solution)/shard_map/all_gather | solution.py:74
  180.7 0.6 copy-start.4
  180.7 1.5 copy-start.3
Sparse Core Ops, SparseCore 0:
  13.0 57.9 all-gather.8
  74.4 54.0 all-gather.10
  182.3 51.1 all-gather.12
